TPU v7x, 128 devices: a whole 4x4x4 slice. The times are simulated.
128 devices in a mesh: fluid: 32 (over x, y, core), solid: 4 (over z).
Axes of the slice: x: 4, y: 4, z: 4, core: 2. Of those that a mesh axis runs over, the one named last changes fastest.
Arguments:
- rbf_blocks: bfloat16 [13312, 256, 256], P(('fluid', 'solid')), may hold values from -0.375 to 0.375
- fluid_traction: bfloat16 [13312, 768], P(('fluid', 'solid')), may hold values from -24 to 24
- fluid_mass: bfloat16 [13312, 768], P(('fluid', 'solid')), may hold values from 0.19921875 to 2
- route: int32 [13312, 1], P(('fluid', 'solid')), may hold values from 0 to 127; in each aligned block of 104 rows (0 to 103, 104 to 207, ...) at most 2 rows name the same one
- slot: int32 [13312], P(('fluid', 'solid')), may hold values from 0 to 7
- shell_inverse: bfloat16 [1024, 768, 768], P(('fluid', 'solid')), may hold values from -0.0078125 to 0.0078125
- robin_coef: float32 [1024, 768], P(('fluid', 'solid')), may hold values from 1 to 27
- shell_start: float32 [1024, 768], P(('fluid', 'solid')), may hold values from -3 to 3
Outputs:
- shell_displacement: float32 [1024, 768], P(('fluid', 'solid'))
- fluid_load: bfloat16 [13312, 768], P(('fluid', 'solid'))
- residual_norms: float32 [6], replicated
Inputs may be any that keep to these rules, and one draw needn't show every extreme that they name: `route`: among the 104 blocks of one device at most 2 name the same owner device.
All inputs are finite; a program needn't handle non-finite values.
Results may differ from a plain program's by a relative error of at most 0.009.
Values may be sent and summed in bfloat16 or wider, within the bound.
No kernel may reach another device: no remote copies, remote signals or barrier semaphores. Data moves between devices by JAX's collectives and lax.ppermute only.
A program may use at most 128 MiB of HBM per device.

v0:
```python
import jax
import jax.numpy as jnp
from jax import lax
from jax.sharding import Mesh
from jax.sharding import PartitionSpec as P

ITERS = 6
FLUID_SOLID = ("fluid_0", "fluid_1", "fluid_2", "solid")
FLUID = ("fluid_0", "fluid_1", "fluid_2")
RELAX = 0.3
EPSILON = 1e-06


def over_axes(array, axes):
    for axis in axes:
        array = lax.psum(array, axis)
    return array


def transport(buffer, devices, capacity):
    breadth = buffer.shape[1]
    moved = lax.all_to_all(
        buffer.reshape(devices, capacity, breadth),
        FLUID_SOLID,
        split_axis=0,
        concat_axis=0,
        tiled=True,
    )
    return moved.reshape(devices * capacity, breadth)


def least_squares(gram, target_side):
    order = gram.shape[0]
    lower = [[None] * order for _ in range(order)]
    for row in range(order):
        for column in range(row + 1):
            total = gram[row, column]
            for inner in range(column):
                total = total - lower[row][inner] * lower[column][inner]
            if row == column:
                lower[row][row] = jnp.sqrt(total)
            else:
                lower[row][column] = total / lower[column][column]
    middle = []
    for row in range(order):
        total = target_side[row]
        for inner in range(row):
            total = total - lower[row][inner] * middle[inner]
        middle.append(total / lower[row][row])
    result = [None] * order
    for row in reversed(range(order)):
        total = middle[row]
        for inner in range(row + 1, order):
            total = total - lower[inner][row] * result[inner]
        result[row] = total / lower[row][row]
    return jnp.stack(result)


def per_device(
    rbf_blocks, fluid_traction, fluid_mass, route, slot, shell_inverse, robin_coef, shell_start
):
    devices = lax.axis_size(FLUID) * lax.axis_size("solid")
    blocks = rbf_blocks.shape[0]
    nodes = rbf_blocks.shape[1]
    breadth = 3 * nodes
    shells = shell_inverse.shape[0]
    capacity = max(2, 2 * blocks // devices)
    slots_all = devices * capacity
    destination = route[:, 0]
    block_order = jnp.arange(blocks, dtype=jnp.int32)
    earlier = (destination[:, None] == destination[None, :]) & (
        block_order[None, :] < block_order[:, None]
    )
    slot_rank = jnp.sum(earlier.astype(jnp.int32), axis=1)
    position = destination * capacity + slot_rank
    positions = jnp.arange(slots_all, dtype=jnp.int32)
    placing = positions[:, None] == position[None, :]
    place_out = placing.astype(jnp.bfloat16)
    place_in = (position[:, None] == positions[None, :]).astype(jnp.bfloat16)
    wanted = jnp.max(jnp.where(placing, slot[None, :] + 1, 0), axis=1) - 1
    asked = lax.all_to_all(
        wanted.reshape(devices, capacity), FLUID_SOLID, split_axis=0, concat_axis=0, tiled=True
    ).reshape(slots_all)
    shell_ids = jnp.arange(shells, dtype=jnp.int32)
    picking = (asked[:, None] == shell_ids[None, :]).astype(jnp.bfloat16)
    collecting = (shell_ids[:, None] == asked[None, :]).astype(jnp.bfloat16)
    traction = fluid_traction.astype(jnp.float32)
    massive = fluid_mass.astype(jnp.float32)
    count = shells * devices * breadth
    current = shell_start
    residuals = []
    images = []
    norms = []
    last_load = None
    for iteration in range(ITERS):
        current_half = current.astype(jnp.bfloat16)
        outgoing = jnp.dot(picking, current_half, preferred_element_type=jnp.float32).astype(
            jnp.bfloat16
        )
        incoming = transport(outgoing, devices, capacity)
        displaced = jnp.dot(place_in, incoming, preferred_element_type=jnp.float32).astype(
            jnp.bfloat16
        )
        moved = jnp.einsum(
            "bcj,bij->bci",
            displaced.reshape(blocks, 3, nodes),
            rbf_blocks,
            preferred_element_type=jnp.float32,
        ).reshape(blocks, breadth)
        load = (traction - massive * moved).astype(jnp.bfloat16)
        last_load = load
        mapped = (
            jnp.einsum(
                "bci,bij->bcj",
                load.reshape(blocks, 3, nodes),
                rbf_blocks,
                preferred_element_type=jnp.float32,
            )
            .reshape(blocks, breadth)
            .astype(jnp.bfloat16)
        )
        sending = jnp.dot(place_out, mapped, preferred_element_type=jnp.float32).astype(
            jnp.bfloat16
        )
        arrived = transport(sending, devices, capacity)
        shell_load = jnp.dot(collecting, arrived, preferred_element_type=jnp.float32)
        forcing = (shell_load + robin_coef * current).astype(jnp.bfloat16)
        image = jnp.einsum("bi,bij->bj", forcing, shell_inverse, preferred_element_type=jnp.float32)
        residual = image - current
        residuals.append(residual)
        images.append(image)
        squares_local = jnp.sum(residual * residual)
        if iteration == 0:
            gram_local = jnp.zeros((1, 1), jnp.float32)
            rhs_local = jnp.zeros((1,), jnp.float32)
        else:
            changes = jnp.stack(
                [(residuals[i + 1] - residuals[i]).reshape(-1) for i in range(iteration)]
            )
            gram_local = jnp.dot(changes, changes.T, precision=lax.Precision.HIGHEST)
            rhs_local = jnp.dot(changes, residual.reshape(-1), precision=lax.Precision.HIGHEST)
        gram, rhs, squares = (
            over_axes(gram_local, FLUID_SOLID),
            over_axes(rhs_local, FLUID_SOLID),
            over_axes(squares_local, FLUID_SOLID),
        )
        norms.append(jnp.sqrt(squares / count + EPSILON))
        if iteration == 0:
            current = current + RELAX * residual
        else:
            image_changes = jnp.stack([images[i + 1] - images[i] for i in range(iteration)])
            coefs = least_squares(gram, -rhs)
            current = image + jnp.tensordot(
                coefs, image_changes, axes=1, precision=lax.Precision.HIGHEST
            )
    return (current, last_load, jnp.stack(norms))


def solution(mesh):
    split = Mesh(
        mesh.devices.reshape(4, 4, 2, mesh.shape["solid"]),
        ("fluid_0", "fluid_1", "fluid_2", "solid"),
    )
    placed = (
        P(FLUID_SOLID, None, None),
        P(FLUID_SOLID, None),
        P(FLUID_SOLID, None),
        P(FLUID_SOLID, None),
        P(FLUID_SOLID),
        P(FLUID_SOLID, None, None),
        P(FLUID_SOLID, None),
        P(FLUID_SOLID, None),
    )
    return jax.shard_map(
        per_device,
        mesh=split,
        in_specs=placed,
        out_specs=(P(FLUID_SOLID, None), P(FLUID_SOLID, None), P()),
        check_vma=False,
    )
```

profile of v0, /device:TPU:0, one launch (start us, length us, event | category | flops | bytes accessed | tf_op | source)
XLA Modules:
  0.0 566.7 jit_solution(6310580616104771973)
XLA Ops:
  2.5 20.0 %all_to_all.66 = s32[128,1,2]{2,1,0:T(1,128)S(1)} all-to-all(s32[128,1,2]{2,1,0:T(1,128)S(1)} %bitcast.371), channel_id=1, replica_groups=mesh['fluid_0'=4,'fluid_1'=4,'fluid_2'=2,'solid'=4] {'fluid_0','fluid_1'..., dimensions={0} | all-to-all | bytes 2048 | tf_op jit(solution)/shard_map/all_to_all | solution.py:81
  33.7 9.0 %all-to-all-done.1 = bf16[128,2,768]{2,1,0:T(2,128)(2,1)S(1)} async-done(((bf16[128,2,768]{2,1,0:T(2,128)(2,1)}), bf16[128,2,768]{2,1,0:T(2,128)(2,1)S(1)}, u32[]{:S(2)}, u32[]{:S(2)}) %all-to-all-start.1) | async-done | bytes 393248 | tf_op jit(solution)/shard_map/all_to_all | solution.py:22
  43.5 8.5 %fusion.118 = f32[104,3,256]{2,1,0:T(4,128)S(1)} fusion(bf16[104,3,256]{2,1,0:T(4,128)(2,1)S(1)} %copy.82, bf16[104,256,256]{2,1,0:T(8,128)(2,1)} %param.8), kind=kOutput, calls=%fused_computation.215 | convolution fusion | flops 40894464 | bytes 14110720 | tf_op jit(solution)/shard_map/bcj,bij->bci/dot_general | solution.py:104
  59.9 16.5 %all_to_all.67 = bf16[128,2,768]{2,1,0:T(2,128)(2,1)S(1)} all-to-all(bf16[128,2,768]{2,1,0:T(2,128)(2,1)S(1)} %reshape.214), channel_id=1, replica_groups=mesh['fluid_0'=4,'fluid_1'=4,'fluid_2'=2,'solid'=4] {'fluid_0','fluid_1'..., dimensions={0} | all-to-all | bytes 786432 | tf_op jit(solution)/shard_map/all_to_all | solution.py:22
  82.3 16.7 %all_to_all.68 = bf16[128,2,768]{2,1,0:T(2,128)(2,1)S(1)} all-to-all(bf16[128,2,768]{2,1,0:T(2,128)(2,1)S(1)} %reshape.216), channel_id=1, replica_groups=mesh['fluid_0'=4,'fluid_1'=4,'fluid_2'=2,'solid'=4] {'fluid_0','fluid_1'..., dimensions={0} | all-to-all | bytes 786432 | tf_op jit(solution)/shard_map/all_to_all | solution.py:22
  99.7 8.5 %fusion.119 = f32[104,3,256]{2,1,0:T(4,128)S(1)} fusion(bf16[104,3,256]{2,1,0:T(4,128)(2,1)S(1)} %copy.87, bf16[104,256,256]{2,1,0:T(8,128)(2,1)} %param.8), kind=kOutput, calls=%fused_computation.216 | convolution fusion | flops 40894464 | bytes 14110720 | tf_op jit(solution)/shard_map/bcj,bij->bci/dot_general | solution.py:104
  116.2 16.5 %all_to_all.69 = bf16[128,2,768]{2,1,0:T(2,128)(2,1)S(1)} all-to-all(bf16[128,2,768]{2,1,0:T(2,128)(2,1)S(1)} %reshape.221), channel_id=1, replica_groups=mesh['fluid_0'=4,'fluid_1'=4,'fluid_2'=2,'solid'=4] {'fluid_0','fluid_1'..., dimensions={0} | all-to-all | bytes 786432 | tf_op jit(solution)/shard_map/all_to_all | solution.py:22
  138.7 9.5 %all-reduce.14 = (f32[1]{0:T(128)}, f32[1,1]{1,0:T(1,128)}) all-reduce(f32[1]{0:T(128)} %bitcast.16, f32[1,1]{1,0:T(1,128)} %bitcast.18), channel_id=1, replica_groups=mesh['fluid_0'=4,'fluid_1'=4,'fluid_2'=2,'solid'=4] {'fluid_0'}, use_global_device_ids=true, to_apply=%region_2.3 | all-reduce | flops 2 | bytes 16 | tf_op jit(solution)/shard_map/psum | solution.py:16
  148.2 9.6 %all-reduce.9 = (f32[1]{0:T(128)}, f32[1,1]{1,0:T(1,128)}) all-reduce(f32[1]{0:T(128)} %get-tuple-element.62, f32[1,1]{1,0:T(1,128)} %get-tuple-element.63), channel_id=1, replica_groups=mesh['fluid_0'=4,'fluid_1'=4,'fluid_2'=2,'solid'=4] {'fluid_1'}, use_global_device_ids=true, to_apply=%region_3.4 | all-reduce | flops 2 | bytes 16 | tf_op jit(solution)/shard_map/psum | solution.py:16
  160.9 9.2 %all-reduce.4 = (f32[1]{0:T(128)}, f32[1,1]{1,0:T(1,128)}) all-reduce(f32[1]{0:T(128)} %get-tuple-element.78, f32[1,1]{1,0:T(1,128)} %get-tuple-element.79), channel_id=1, replica_groups=mesh['fluid_0'=4,'fluid_1'=4,'fluid_2'=2,'solid'=4] {'solid'}, use_global_device_ids=true, to_apply=%region_5.6 | all-reduce | flops 2 | bytes 16 | tf_op jit(solution)/shard_map/psum | solution.py:16
  172.0 16.3 %all_to_all.70 = bf16[128,2,768]{2,1,0:T(2,128)(2,1)S(1)} all-to-all(bf16[128,2,768]{2,1,0:T(2,128)(2,1)S(1)} %reshape.224), channel_id=1, replica_groups=mesh['fluid_0'=4,'fluid_1'=4,'fluid_2'=2,'solid'=4] {'fluid_0','fluid_1'..., dimensions={0} | all-to-all | bytes 786432 | tf_op jit(solution)/shard_map/all_to_all | solution.py:22
  189.0 8.5 %fusion.120 = f32[104,3,256]{2,1,0:T(4,128)S(1)} fusion(bf16[104,3,256]{2,1,0:T(4,128)(2,1)S(1)} %copy.92, bf16[104,256,256]{2,1,0:T(8,128)(2,1)} %param.8), kind=kOutput, calls=%fused_computation.217 | convolution fusion | flops 40894464 | bytes 14110720 | tf_op jit(solution)/shard_map/bcj,bij->bci/dot_general | solution.py:104
  211.0 11.9 %all-to-all-done.6 = bf16[128,2,768]{2,1,0:T(2,128)(2,1)S(1)} async-done(((bf16[128,2,768]{2,1,0:T(2,128)(2,1)}), bf16[128,2,768]{2,1,0:T(2,128)(2,1)S(1)}, u32[]{:S(2)}, u32[]{:S(2)}) %all-to-all-start.6) | async-done | bytes 393248 | tf_op jit(solution)/shard_map/all_to_all | solution.py:22
  230.0 8.9 %all-reduce.13 = (f32[2]{0:T(128)S(1)}, f32[2,2]{1,0:T(2,128)S(1)}) all-reduce(f32[2]{0:T(128)S(1)} %convolution_bitcast_fusion.3, f32[2,2]{1,0:T(2,128)S(1)} %fusion.69), channel_id=1, replica_groups=mesh['fluid_0'=4,'fluid_1'=4,'fluid_2'=2,'solid'=4] {'fluid_0'}, use_global_device_ids=true, to_apply=%region_10.11 | all-reduce | flops 6 | bytes 48 | tf_op jit(solution)/shard_map/psum | solution.py:16
  238.9 9.0 %all-reduce.8 = (f32[2]{0:T(128)S(1)}, f32[2,2]{1,0:T(2,128)S(1)}) all-reduce(f32[2]{0:T(128)S(1)} %get-tuple-element.60, f32[2,2]{1,0:T(2,128)S(1)} %get-tuple-element.61), channel_id=1, replica_groups=mesh['fluid_0'=4,'fluid_1'=4,'fluid_2'=2,'solid'=4] {'fluid_1'}, use_global_device_ids=true, to_apply=%region_11.12 | all-reduce | flops 6 | bytes 48 | tf_op jit(solution)/shard_map/psum | solution.py:16
  250.3 8.6 %all-reduce.3 = (f32[2]{0:T(128)S(1)}, f32[2,2]{1,0:T(2,128)S(1)}) all-reduce(f32[2]{0:T(128)S(1)} %get-tuple-element.76, f32[2,2]{1,0:T(2,128)S(1)} %get-tuple-element.77), channel_id=1, replica_groups=mesh['fluid_0'=4,'fluid_1'=4,'fluid_2'=2,'solid'=4] {'solid'}, use_global_device_ids=true, to_apply=%region_13.14 | all-reduce | flops 6 | bytes 48 | tf_op jit(solution)/shard_map/psum | solution.py:16
  264.3 16.0 %all_to_all.71 = bf16[128,2,768]{2,1,0:T(2,128)(2,1)S(1)} all-to-all(bf16[128,2,768]{2,1,0:T(2,128)(2,1)S(1)} %reshape.232), channel_id=1, replica_groups=mesh['fluid_0'=4,'fluid_1'=4,'fluid_2'=2,'solid'=4] {'fluid_0','fluid_1'..., dimensions={0} | all-to-all | bytes 786432 | tf_op jit(solution)/shard_map/all_to_all | solution.py:22
  297.6 16.5 %all_to_all.72 = bf16[128,2,768]{2,1,0:T(2,128)(2,1)S(1)} all-to-all(bf16[128,2,768]{2,1,0:T(2,128)(2,1)S(1)} %reshape.237), channel_id=1, replica_groups=mesh['fluid_0'=4,'fluid_1'=4,'fluid_2'=2,'solid'=4] {'fluid_0','fluid_1'..., dimensions={0} | all-to-all | bytes 786432 | tf_op jit(solution)/shard_map/all_to_all | solution.py:22
  321.2 8.9 %all-reduce.12 = (f32[3]{0:T(128)S(1)}, f32[3,3]{1,0:T(4,128)S(1)}) all-reduce(f32[3]{0:T(128)S(1)} %convolution_bitcast_fusion.2, f32[3,3]{1,0:T(4,128)S(1)} %fusion.49), channel_id=1, replica_groups=mesh['fluid_0'=4,'fluid_1'=4,'fluid_2'=2,'solid'=4] {'fluid_0'}, use_global_device_ids=true, to_apply=%region_18.19 | all-reduce | flops 12 | bytes 96 | tf_op jit(solution)/shard_map/psum | solution.py:16
  330.0 9.0 %all-reduce.7 = (f32[3]{0:T(128)S(1)}, f32[3,3]{1,0:T(4,128)S(1)}) all-reduce(f32[3]{0:T(128)S(1)} %get-tuple-element.58, f32[3,3]{1,0:T(4,128)S(1)} %get-tuple-element.59), channel_id=1, replica_groups=mesh['fluid_0'=4,'fluid_1'=4,'fluid_2'=2,'solid'=4] {'fluid_1'}, use_global_device_ids=true, to_apply=%region_19.20 | all-reduce | flops 12 | bytes 96 | tf_op jit(solution)/shard_map/psum | solution.py:16
  341.4 8.6 %all-reduce.2 = (f32[3]{0:T(128)S(1)}, f32[3,3]{1,0:T(4,128)S(1)}) all-reduce(f32[3]{0:T(128)S(1)} %get-tuple-element.74, f32[3,3]{1,0:T(4,128)S(1)} %get-tuple-element.75), channel_id=1, replica_groups=mesh['fluid_0'=4,'fluid_1'=4,'fluid_2'=2,'solid'=4] {'solid'}, use_global_device_ids=true, to_apply=%region_21.22 | all-reduce | flops 12 | bytes 96 | tf_op jit(solution)/shard_map/psum | solution.py:16
  358.3 16.1 %all_to_all.73 = bf16[128,2,768]{2,1,0:T(2,128)(2,1)S(1)} all-to-all(bf16[128,2,768]{2,1,0:T(2,128)(2,1)S(1)} %reshape.240), channel_id=1, replica_groups=mesh['fluid_0'=4,'fluid_1'=4,'fluid_2'=2,'solid'=4] {'fluid_0','fluid_1'..., dimensions={0} | all-to-all | bytes 786432 | tf_op jit(solution)/shard_map/all_to_all | solution.py:22
  375.1 8.5 %fusion.122 = f32[104,3,256]{2,1,0:T(4,128)S(1)} fusion(bf16[104,3,256]{2,1,0:T(4,128)(2,1)S(1)} %copy.102, bf16[104,256,256]{2,1,0:T(8,128)(2,1)} %param.8), kind=kOutput, calls=%fused_computation.219 | convolution fusion | flops 40894464 | bytes 14110720 | tf_op jit(solution)/shard_map/bcj,bij->bci/dot_general | solution.py:104
  391.5 16.5 %all_to_all.74 = bf16[128,2,768]{2,1,0:T(2,128)(2,1)S(1)} all-to-all(bf16[128,2,768]{2,1,0:T(2,128)(2,1)S(1)} %reshape.245), channel_id=1, replica_groups=mesh['fluid_0'=4,'fluid_1'=4,'fluid_2'=2,'solid'=4] {'fluid_0','fluid_1'..., dimensions={0} | all-to-all | bytes 786432 | tf_op jit(solution)/shard_map/all_to_all | solution.py:22
  415.2 8.9 %all-reduce.11 = (f32[4]{0:T(128)S(1)}, f32[4,4]{1,0:T(4,128)S(1)}) all-reduce(f32[4]{0:T(128)S(1)} %convolution_bitcast_fusion.1, f32[4,4]{1,0:T(4,128)S(1)} %fusion.68), channel_id=1, replica_groups=mesh['fluid_0'=4,'fluid_1'=4,'fluid_2'=2,'solid'=4] {'fluid_0'}, use_global_device_ids=true, to_apply=%region_26.27 | all-reduce | flops 20 | bytes 160 | tf_op jit(solution)/shard_map/psum | solution.py:16
  424.1 9.0 %all-reduce.6 = (f32[4]{0:T(128)S(1)}, f32[4,4]{1,0:T(4,128)S(1)}) all-reduce(f32[4]{0:T(128)S(1)} %get-tuple-element.56, f32[4,4]{1,0:T(4,128)S(1)} %get-tuple-element.57), channel_id=1, replica_groups=mesh['fluid_0'=4,'fluid_1'=4,'fluid_2'=2,'solid'=4] {'fluid_1'}, use_global_device_ids=true, to_apply=%region_27.28 | all-reduce | flops 20 | bytes 160 | tf_op jit(solution)/shard_map/psum | solution.py:16
  435.5 8.6 %all-reduce.1 = (f32[4]{0:T(128)S(1)}, f32[4,4]{1,0:T(4,128)S(1)}) all-reduce(f32[4]{0:T(128)S(1)} %get-tuple-element.72, f32[4,4]{1,0:T(4,128)S(1)} %get-tuple-element.73), channel_id=1, replica_groups=mesh['fluid_0'=4,'fluid_1'=4,'fluid_2'=2,'solid'=4] {'solid'}, use_global_device_ids=true, to_apply=%region_29.30 | all-reduce | flops 20 | bytes 160 | tf_op jit(solution)/shard_map/psum | solution.py:16
  455.7 16.1 %all_to_all.75 = bf16[128,2,768]{2,1,0:T(2,128)(2,1)S(1)} all-to-all(bf16[128,2,768]{2,1,0:T(2,128)(2,1)S(1)} %reshape.248), channel_id=1, replica_groups=mesh['fluid_0'=4,'fluid_1'=4,'fluid_2'=2,'solid'=4] {'fluid_0','fluid_1'..., dimensions={0} | all-to-all | bytes 786432 | tf_op jit(solution)/shard_map/all_to_all | solution.py:22
  495.4 11.1 %all-to-all-done.12 = bf16[128,2,768]{2,1,0:T(2,128)(2,1)S(1)} async-done(((bf16[128,2,768]{2,1,0:T(2,128)(2,1)}), bf16[128,2,768]{2,1,0:T(2,128)(2,1)S(1)}, u32[]{:S(2)}, u32[]{:S(2)}) %all-to-all-start.12) | async-done | bytes 393248 | tf_op jit(solution)/shard_map/all_to_all | solution.py:22
  513.8 9.7 %all-reduce.10 = (f32[5]{0:T(128)S(1)}, f32[5,5]{1,0:T(8,128)S(1)}, f32[]{:T(128)}, f32[]{:T(128)}, f32[]{:T(128)}, /*index=5*/f32[]{:T(128)}, f32[]{:T(128)}, f32[]{:T(128)}) all-reduce(f32[5]{0:T(128)S(1)} %convolution_bitcast_fusion, ...), channel_id=1, replica_groups=mesh['fluid_0'=4,'fluid_1'=4,'fluid_2'=2,'solid'=4] {'fluid_0'}, use_global_device_ids=true, to_apply=%region_34.35 | all-reduce | flops 36 | bytes 288 | tf_op jit(solution)/shard_map/psum | solution.py:16
  523.5 9.8 %all-reduce.5 = (f32[5]{0:T(128)S(1)}, f32[5,5]{1,0:T(8,128)S(1)}, f32[]{:T(128)}, f32[]{:T(128)}, f32[]{:T(128)}, /*index=5*/f32[]{:T(128)}, f32[]{:T(128)}, f32[]{:T(128)}) all-reduce(f32[5]{0:T(128)S(1)} %get-tuple-element.48, ...), channel_id=1, replica_groups=mesh['fluid_0'=4,'fluid_1'=4,'fluid_2'=2,'solid'=4] {'fluid_1'}, use_global_device_ids=true, to_apply=%region_35.36 | all-reduce | flops 36 | bytes 288 | tf_op jit(solution)/shard_map/psum | solution.py:16
  536.5 9.4 %all-reduce = (f32[5]{0:T(128)S(1)}, f32[5,5]{1,0:T(8,128)S(1)}, f32[]{:T(128)}, f32[]{:T(128)}, f32[]{:T(128)}, /*index=5*/f32[]{:T(128)}, f32[]{:T(128)}, f32[]{:T(128)}) all-reduce(f32[5]{0:T(128)S(1)} %get-tuple-element.64, ...), channel_id=1, replica_groups=mesh['fluid_0'=4,'fluid_1'=4,'fluid_2'=2,'solid'=4] {'solid'}, use_global_device_ids=true, to_apply=%region_37.38 | all-reduce | flops 36 | bytes 288 | tf_op jit(solution)/shard_map/psum | solution.py:16
  (179 shorter events, 157.8 us)
Async XLA Ops:
  25.9 16.8 %all-to-all-start.1 = ((bf16[128,2,768]{2,1,0:T(2,128)(2,1)}), bf16[128,2,768]{2,1,0:T(2,128)(2,1)S(1)}, u32[]{:S(2)}, u32[]{:S(2)}) async-start(bf16[128,2,768]{2,1,0:T(2,128)(2,1)} %reshape.209), calls=%async_computation.1 | async-start | bytes 786432 | tf_op jit(solution)/shard_map/all_to_all | solution.py:22
  52.1 24.4 %copy-start = (f32[8,768]{1,0:T(8,128)S(1)}, f32[8,768]{1,0:T(8,128)}, u32[]{:S(2)}) copy-start(f32[8,768]{1,0:T(8,128)} %param.14) | copy-start | bytes 73732
  52.2 24.4 %copy-start.1 = (f32[8,768]{1,0:T(8,128)S(1)}, f32[8,768]{1,0:T(8,128)}, u32[]{:S(2)}) copy-start(f32[8,768]{1,0:T(8,128)} %param.15) | copy-start | bytes 73732
  206.1 16.7 %all-to-all-start.6 = ((bf16[128,2,768]{2,1,0:T(2,128)(2,1)}), bf16[128,2,768]{2,1,0:T(2,128)(2,1)S(1)}, u32[]{:S(2)}, u32[]{:S(2)}) async-start(bf16[128,2,768]{2,1,0:T(2,128)(2,1)} %reshape.229), calls=%async_computation.6 | async-start | bytes 786432 | tf_op jit(solution)/shard_map/all_to_all | solution.py:22
  489.8 16.7 %all-to-all-start.12 = ((bf16[128,2,768]{2,1,0:T(2,128)(2,1)}), bf16[128,2,768]{2,1,0:T(2,128)(2,1)S(1)}, u32[]{:S(2)}, u32[]{:S(2)}) async-start(bf16[128,2,768]{2,1,0:T(2,128)(2,1)} %reshape.253), calls=%async_computation.12 | async-start | bytes 786432 | tf_op jit(solution)/shard_map/all_to_all | solution.py:22
where the time goes:
time: 576 us; the launch traced here: 567 us
  blocking collectives  317 us (55%)
  matrix products  134 us (23%)
  between operations  39.4 us (7%)
  waiting for transfers between devices  32 us (6%)
  local copies, waits for them, and re-layouts  21.6 us (4%)
  starting transfers between devices  14.5 us (3%)
  other arithmetic  7.59 us (1%)
    psum x20, blocking collectives, over_axes(): array = lax.psum(array, axis)  150 us
    all_to_all x9, blocking collectives, transport(): lax.all_to_all(buffer.reshape(devices, capacity, breadth), FLUID_SOLID, s...  147 us
    dot_general x6, matrix products, per_device(): jnp.einsum('bcj,bij->bci', displaced.reshape(blocks, 3, nodes), rbf_block...  50.9 us
    dot_general x6, matrix products, per_device(): jnp.einsum('bci,bij->bcj', load.reshape(blocks, 3, nodes), rbf_blocks, pr...  40.5 us
    all_to_all x3, waiting for transfers between devices, transport(): lax.all_to_all(buffer.reshape(devices, capacity, breadth), FLUID_SOLID, s...  32 us
    dot_general x6, matrix products, per_device(): jnp.einsum('bi,bij->bj', forcing, shell_inverse, preferred_element_type=j...  30.1 us
    all_to_all x1, blocking collectives, per_device(): lax.all_to_all(wanted.reshape(devices, capacity), FLUID_SOLID, split_axis...  20 us
    all_to_all x3, starting transfers between devices, transport(): lax.all_to_all(buffer.reshape(devices, capacity, breadth), FLUID_SOLID, s...  14.5 us
  transfers between devices with their start and end apart: 3, of which 3 were waited for; matrix products, arithmetic and copies ran while one was open for 1% of the time, Pallas kernels for 0%

commit v1 on v0

--- a/solution.py
+++ b/solution.py
@@ -13,7 +13,7 @@
 
 def over_axes(array, axes):
     for axis in axes:
-        array = lax.psum(array, axis)
+        array = lax.all_gather(array, axis).sum(axis=0)
     return array
 
 

time: 576 us -> 779 us (1.35)
  blocking collectives: 317 us -> 403 us
  local copies, waits for them, and re-layouts: 21.6 us -> 76.3 us
  other arithmetic: 7.59 us -> 27.5 us
  waiting for transfers between devices: 32 us -> 49.8 us
  starting transfers between devices: 14.5 us -> 28.9 us
  between operations: 39.4 us -> 49.4 us
    psum x20 -> x0, blocking collectives: 150 us -> none  [over_axes(): array = lax.psum(array, axis)]
    unnamed x0 -> x20, blocking collectives: none -> 148 us
    all_gather x0 -> x16, blocking collectives: none -> 129 us  [over_axes(): array = lax.all_gather(array, axis).sum(axis=0)]
    unnamed x16 -> x124, local copies, waits for them, and re-layouts: 3.25 us -> 54.2 us
    all_to_all x9 -> x6, blocking collectives: 147 us -> 106 us  [transport(): lax.all_to_all(buffer.reshape(devices, capacity, breadth), FLUID_SOLID, s...]
    reduce_sum x0 -> x64, other arithmetic: none -> 20 us  [over_axes(): array = lax.all_gather(array, axis).sum(axis=0)]
    all_to_all x3 -> x6, waiting for transfers between devices: 32 us -> 49.8 us  [transport(): lax.all_to_all(buffer.reshape(devices, capacity, breadth), FLUID_SOLID, s...]
    all_to_all x3 -> x6, starting transfers between devices: 14.5 us -> 28.9 us  [transport(): lax.all_to_all(buffer.reshape(devices, capacity, breadth), FLUID_SOLID, s...]
  transfers between devices with their start and end apart: 3 -> 6, of which waited for: 3 -> 6; matrix products, arithmetic and copies ran while one was open for 1% -> 1% of each run, Pallas kernels for 0% -> 0%
where the time goes in v1:
time: 779 us; the launch traced here: 769 us
  blocking collectives  403 us (52%)
  matrix products  134 us (17%)
  local copies, waits for them, and re-layouts  76.3 us (10%)
  waiting for transfers between devices  49.8 us (6%)
  between operations  49.4 us (6%)
  starting transfers between devices  28.9 us (4%)
  other arithmetic  27.5 us (4%)
    unnamed x20, blocking collectives  148 us
    all_gather x16, blocking collectives, over_axes(): array = lax.all_gather(array, axis).sum(axis=0)  129 us
    all_to_all x6, blocking collectives, transport(): lax.all_to_all(buffer.reshape(devices, capacity, breadth), FLUID_SOLID, s...  106 us
    unnamed x124, local copies, waits for them, and re-layouts  54.2 us
    dot_general x6, matrix products, per_device(): jnp.einsum('bcj,bij->bci', displaced.reshape(blocks, 3, nodes), rbf_block...  50.9 us
    all_to_all x6, waiting for transfers between devices, transport(): lax.all_to_all(buffer.reshape(devices, capacity, breadth), FLUID_SOLID, s...  49.8 us
    dot_general x6, matrix products, per_device(): jnp.einsum('bci,bij->bcj', load.reshape(blocks, 3, nodes), rbf_blocks, pr...  40.5 us
    dot_general x6, matrix products, per_device(): jnp.einsum('bi,bij->bj', forcing, shell_inverse, preferred_element_type=j...  30.1 us
  transfers between devices with their start and end apart: 6, of which 6 were waited for; matrix products, arithmetic and copies ran while one was open for 1% of the time, Pallas kernels for 0%

profile of v1, /device:TPU:0, one launch (start us, length us, event | category | flops | bytes accessed | tf_op | source)
XLA Modules:
  0.0 768.8 jit_solution(12957888353246251935)
XLA Ops:
  2.5 20.0 %all_to_all.66 = s32[128,1,2]{2,1,0:T(1,128)S(1)} all-to-all(s32[128,1,2]{2,1,0:T(1,128)S(1)} %bitcast.439), channel_id=1, replica_groups=mesh['fluid_0'=4,'fluid_1'=4,'fluid_2'=2,'solid'=4] {'fluid_0','fluid_1'..., dimensions={0} | all-to-all | bytes 2048 | tf_op jit(solution)/shard_map/all_to_all | solution.py:81
  33.7 9.0 %all-to-all-done.1 = bf16[128,2,768]{2,1,0:T(2,128)(2,1)S(1)} async-done(((bf16[128,2,768]{2,1,0:T(2,128)(2,1)}), bf16[128,2,768]{2,1,0:T(2,128)(2,1)S(1)}, u32[]{:S(2)}, u32[]{:S(2)}) %all-to-all-start.1) | async-done | bytes 393248 | tf_op jit(solution)/shard_map/all_to_all | solution.py:22
  59.9 16.5 %all_to_all.67 = bf16[128,2,768]{2,1,0:T(2,128)(2,1)S(1)} all-to-all(bf16[128,2,768]{2,1,0:T(2,128)(2,1)S(1)} %reshape.229), channel_id=1, replica_groups=mesh['fluid_0'=4,'fluid_1'=4,'fluid_2'=2,'solid'=4] {'fluid_0','fluid_1'..., dimensions={0} | all-to-all | bytes 786432 | tf_op jit(solution)/shard_map/all_to_all | solution.py:22
  82.3 16.8 %all_to_all.68 = bf16[128,2,768]{2,1,0:T(2,128)(2,1)S(1)} all-to-all(bf16[128,2,768]{2,1,0:T(2,128)(2,1)S(1)} %reshape.231), channel_id=1, replica_groups=mesh['fluid_0'=4,'fluid_1'=4,'fluid_2'=2,'solid'=4] {'fluid_0','fluid_1'..., dimensions={0} | all-to-all | bytes 786432 | tf_op jit(solution)/shard_map/all_to_all | solution.py:22
  122.5 11.2 %all-to-all-done.4 = bf16[128,2,768]{2,1,0:T(2,128)(2,1)S(1)} async-done(((bf16[128,2,768]{2,1,0:T(2,128)(2,1)}), bf16[128,2,768]{2,1,0:T(2,128)(2,1)S(1)}, u32[]{:S(2)}, u32[]{:S(2)}) %all-to-all-start.4) | async-done | bytes 393248 | tf_op jit(solution)/shard_map/all_to_all | solution.py:22
  143.0 8.8 %all-reduce.53 = (f32[4]{0:T(128)S(1)}, f32[4]{0:T(128)S(1)}) all-reduce(f32[4]{0:T(128)S(1)} %dynamic-update-slice, f32[4]{0:T(128)S(1)} %dynamic-update-slice.4), channel_id=1, replica_groups=mesh['fluid_0'=4,'fluid_1'=4,'fluid_2'=2,'solid'=4] {'fluid_0'}, use_global_device_ids=true, to_apply=%add | all-reduce | flops 8 | bytes 64
  156.5 8.9 %all-reduce.51 = (f32[4]{0:T(128)S(1)}, f32[4]{0:T(128)S(1)}) all-reduce(f32[4]{0:T(128)S(1)} %dynamic-update-slice.1, f32[4]{0:T(128)S(1)} %dynamic-update-slice.5), channel_id=1, replica_groups=mesh['fluid_0'=4,'fluid_1'=4,'fluid_2'=2,'solid'=4] {'fluid_1'}, use_global_device_ids=true, to_apply=%add.1 | all-reduce | flops 8 | bytes 64
  188.5 16.4 %all_to_all.69 = bf16[128,2,768]{2,1,0:T(2,128)(2,1)S(1)} all-to-all(bf16[128,2,768]{2,1,0:T(2,128)(2,1)S(1)} %reshape.238), channel_id=1, replica_groups=mesh['fluid_0'=4,'fluid_1'=4,'fluid_2'=2,'solid'=4] {'fluid_0','fluid_1'..., dimensions={0} | all-to-all | bytes 786432 | tf_op jit(solution)/shard_map/all_to_all | solution.py:22
  230.2 9.3 %all-to-all-done.6 = bf16[128,2,768]{2,1,0:T(2,128)(2,1)S(1)} async-done(((bf16[128,2,768]{2,1,0:T(2,128)(2,1)}), bf16[128,2,768]{2,1,0:T(2,128)(2,1)S(1)}, u32[]{:S(2)}, u32[]{:S(2)}) %all-to-all-start.6) | async-done | bytes 393248 | tf_op jit(solution)/shard_map/all_to_all | solution.py:22
  246.3 8.9 %all-reduce.8 = f32[8]{0:T(128)S(1)} all-reduce(f32[8]{0:T(128)S(1)} %dynamic-update-slice.8), channel_id=2, replica_groups=mesh['fluid_0'=4,'fluid_1'=4,'fluid_2'=2,'solid'=4] {'fluid_0'}, use_global_device_ids=true, to_apply=%add.8 | all-reduce | flops 8 | bytes 64
  255.5 9.0 %all-reduce.9 = f32[8]{0:T(128)S(1)} all-reduce(f32[8]{0:T(128)S(1)} %dynamic-update-slice.9), channel_id=3, replica_groups=mesh['fluid_0'=4,'fluid_1'=4,'fluid_2'=2,'solid'=4] {'fluid_1'}, use_global_device_ids=true, to_apply=%add.9 | all-reduce | flops 8 | bytes 64
  307.8 16.0 %all_to_all.70 = bf16[128,2,768]{2,1,0:T(2,128)(2,1)S(1)} all-to-all(bf16[128,2,768]{2,1,0:T(2,128)(2,1)S(1)} %reshape.246), channel_id=1, replica_groups=mesh['fluid_0'=4,'fluid_1'=4,'fluid_2'=2,'solid'=4] {'fluid_0','fluid_1'..., dimensions={0} | all-to-all | bytes 786432 | tf_op jit(solution)/shard_map/all_to_all | solution.py:22
  349.2 9.3 %all-to-all-done.8 = bf16[128,2,768]{2,1,0:T(2,128)(2,1)S(1)} async-done(((bf16[128,2,768]{2,1,0:T(2,128)(2,1)}), bf16[128,2,768]{2,1,0:T(2,128)(2,1)S(1)}, u32[]{:S(2)}, u32[]{:S(2)}) %all-to-all-start.8) | async-done | bytes 393248 | tf_op jit(solution)/shard_map/all_to_all | solution.py:22
  365.3 8.9 %all-reduce.12 = f32[12]{0:T(128)S(1)} all-reduce(f32[12]{0:T(128)S(1)} %dynamic-update-slice.12), channel_id=10, replica_groups=mesh['fluid_0'=4,'fluid_1'=4,'fluid_2'=2,'solid'=4] {'fluid_0'}, use_global_device_ids=true, to_apply=%add.12 | all-reduce | flops 12 | bytes 96
  374.5 8.9 %all-reduce.13 = f32[12]{0:T(128)S(1)} all-reduce(f32[12]{0:T(128)S(1)} %dynamic-update-slice.13), channel_id=11, replica_groups=mesh['fluid_0'=4,'fluid_1'=4,'fluid_2'=2,'solid'=4] {'fluid_1'}, use_global_device_ids=true, to_apply=%add.13 | all-reduce | flops 12 | bytes 96
  396.5 10.4 %all-gather.36 = f32[4,3,3]{2,1,0:T(4,128)S(1)} all-gather(f32[1,3,3]{2,1,0:T(4,128)S(1)} %convolution_bitcast_fusion.2), channel_id=14, replica_groups=mesh['fluid_0'=4,'fluid_1'=4,'fluid_2'=2,'solid'=4] {'fluid_0'}, dimensions={0}, use_global_device_ids=true | all-gather | bytes 180 | tf_op jit(solution)/shard_map/all_gather | solution.py:16
  406.9 10.4 %all-gather.37 = f32[4,3,3]{2,1,0:T(4,128)S(1)} all-gather(f32[1,3,3]{2,1,0:T(4,128)S(1)} %bitcast.472), channel_id=15, replica_groups=mesh['fluid_0'=4,'fluid_1'=4,'fluid_2'=2,'solid'=4] {'fluid_1'}, dimensions={0}, use_global_device_ids=true | all-gather | bytes 180 | tf_op jit(solution)/shard_map/all_gather | solution.py:16
  419.1 10.4 %all-gather.39 = f32[4,3,3]{2,1,0:T(4,128)S(1)} all-gather(f32[1,3,3]{2,1,0:T(4,128)S(1)} %bitcast.470), channel_id=17, replica_groups=mesh['fluid_0'=4,'fluid_1'=4,'fluid_2'=2,'solid'=4] {'solid'}, dimensions={0}, use_global_device_ids=true | all-gather | bytes 180 | tf_op jit(solution)/shard_map/all_gather | solution.py:16
  437.0 20.0 %all_to_all.71 = bf16[128,2,768]{2,1,0:T(2,128)(2,1)S(1)} all-to-all(bf16[128,2,768]{2,1,0:T(2,128)(2,1)S(1)} %reshape.254), channel_id=1, replica_groups=mesh['fluid_0'=4,'fluid_1'=4,'fluid_2'=2,'solid'=4] {'fluid_0','fluid_1'..., dimensions={0} | all-to-all | bytes 786432 | tf_op jit(solution)/shard_map/all_to_all | solution.py:22
  482.3 9.3 %all-to-all-done.10 = bf16[128,2,768]{2,1,0:T(2,128)(2,1)S(1)} async-done(((bf16[128,2,768]{2,1,0:T(2,128)(2,1)}), bf16[128,2,768]{2,1,0:T(2,128)(2,1)S(1)}, u32[]{:S(2)}, u32[]{:S(2)}) %all-to-all-start.10) | async-done | bytes 393248 | tf_op jit(solution)/shard_map/all_to_all | solution.py:22
  498.4 8.9 %all-reduce.16 = f32[16]{0:T(128)S(1)} all-reduce(f32[16]{0:T(128)S(1)} %dynamic-update-slice.16), channel_id=18, replica_groups=mesh['fluid_0'=4,'fluid_1'=4,'fluid_2'=2,'solid'=4] {'fluid_0'}, use_global_device_ids=true, to_apply=%add.16 | all-reduce | flops 16 | bytes 128
  507.6 8.9 %all-reduce.17 = f32[16]{0:T(128)S(1)} all-reduce(f32[16]{0:T(128)S(1)} %dynamic-update-slice.17), channel_id=19, replica_groups=mesh['fluid_0'=4,'fluid_1'=4,'fluid_2'=2,'solid'=4] {'fluid_1'}, use_global_device_ids=true, to_apply=%add.17 | all-reduce | flops 16 | bytes 128
  529.6 10.4 %all-gather.40 = f32[4,4,4]{2,1,0:T(4,128)S(1)} all-gather(f32[1,4,4]{2,1,0:T(4,128)S(1)} %convolution_bitcast_fusion.1), channel_id=22, replica_groups=mesh['fluid_0'=4,'fluid_1'=4,'fluid_2'=2,'solid'=4] {'fluid_0'}, dimensions={0}, use_global_device_ids=true | all-gather | bytes 320 | tf_op jit(solution)/shard_map/all_gather | solution.py:16
  540.0 10.4 %all-gather.41 = f32[4,4,4]{2,1,0:T(4,128)S(1)} all-gather(f32[1,4,4]{2,1,0:T(4,128)S(1)} %bitcast.474), channel_id=23, replica_groups=mesh['fluid_0'=4,'fluid_1'=4,'fluid_2'=2,'solid'=4] {'fluid_1'}, dimensions={0}, use_global_device_ids=true | all-gather | bytes 320 | tf_op jit(solution)/shard_map/all_gather | solution.py:16
  552.2 10.4 %all-gather.43 = f32[4,4,4]{2,1,0:T(4,128)S(1)} all-gather(f32[1,4,4]{2,1,0:T(4,128)S(1)} %bitcast.471), channel_id=25, replica_groups=mesh['fluid_0'=4,'fluid_1'=4,'fluid_2'=2,'solid'=4] {'solid'}, dimensions={0}, use_global_device_ids=true | all-gather | bytes 320 | tf_op jit(solution)/shard_map/all_gather | solution.py:16
  573.5 20.1 %all_to_all.72 = bf16[128,2,768]{2,1,0:T(2,128)(2,1)S(1)} all-to-all(bf16[128,2,768]{2,1,0:T(2,128)(2,1)S(1)} %reshape.262), channel_id=1, replica_groups=mesh['fluid_0'=4,'fluid_1'=4,'fluid_2'=2,'solid'=4] {'fluid_0','fluid_1'..., dimensions={0} | all-to-all | bytes 786432 | tf_op jit(solution)/shard_map/all_to_all | solution.py:22
  636.6 8.9 %all-reduce.52 = (f32[20]{0:T(128)S(1)}, f32[4]{0:T(128)S(1)}, f32[4]{0:T(128)S(1)}, f32[4]{0:T(128)S(1)}, f32[4]{0:T(128)S(1)}, /*index=5*/f32[4]{0:T(128)S(1)}, f32[4]{0:T(128)S(1)}) all-reduce(f32[20]{0:T(128)S(1)} %dynamic-update-slice.20, ...), channel_id=26, replica_groups=mesh['fluid_0'=4,'fluid_1'=4,'fluid_2'=2,'solid'=4] {'fluid_0'}, use_global_device_ids=true, to_apply=%add.20 | all-reduce | flops 44 | bytes 352
  657.8 9.9 %all-reduce.50 = (f32[20]{0:T(128)S(1)}, f32[4]{0:T(128)S(1)}, f32[4]{0:T(128)S(1)}, f32[4]{0:T(128)S(1)}, f32[4]{0:T(128)S(1)}, /*index=5*/f32[4]{0:T(128)S(1)}, f32[4]{0:T(128)S(1)}) all-reduce(f32[20]{0:T(128)S(1)} %dynamic-update-slice.21, ...), channel_id=27, replica_groups=mesh['fluid_0'=4,'fluid_1'=4,'fluid_2'=2,'solid'=4] {'fluid_1'}, use_global_device_ids=true, to_apply=%add.21 | all-reduce | flops 44 | bytes 352
  695.6 11.2 %all-reduce.48 = (f32[20]{0:T(128)S(1)}, f32[4]{0:T(128)S(1)}, f32[4]{0:T(128)S(1)}, f32[4]{0:T(128)S(1)}, f32[4]{0:T(128)S(1)}, /*index=5*/f32[4]{0:T(128)S(1)}, f32[4]{0:T(128)S(1)}) all-reduce(f32[20]{0:T(128)S(1)} %dynamic-update-slice.23, ...), channel_id=29, replica_groups=mesh['fluid_0'=4,'fluid_1'=4,'fluid_2'=2,'solid'=4] {'solid'}, use_global_device_ids=true, to_apply=%add.23 | all-reduce | flops 44 | bytes 352
  707.6 11.9 %all-gather.44 = f32[4,5,5]{2,1,0:T(8,128)S(1)} all-gather(f32[1,5,5]{2,1,0:T(8,128)S(1)} %convolution_bitcast_fusion), channel_id=30, replica_groups=mesh['fluid_0'=4,'fluid_1'=4,'fluid_2'=2,'solid'=4] {'fluid_0'}, dimensions={0}, use_global_device_ids=true | all-gather | bytes 500 | tf_op jit(solution)/shard_map/all_gather | solution.py:16
  719.5 11.9 %all-gather.45 = f32[4,5,5]{2,1,0:T(8,128)S(1)} all-gather(f32[1,5,5]{2,1,0:T(8,128)S(1)} %bitcast.468), channel_id=31, replica_groups=mesh['fluid_0'=4,'fluid_1'=4,'fluid_2'=2,'solid'=4] {'fluid_1'}, dimensions={0}, use_global_device_ids=true | all-gather | bytes 500 | tf_op jit(solution)/shard_map/all_gather | solution.py:16
  733.3 11.9 %all-gather.47 = f32[4,5,5]{2,1,0:T(8,128)S(1)} all-gather(f32[1,5,5]{2,1,0:T(8,128)S(1)} %bitcast.467), channel_id=33, replica_groups=mesh['fluid_0'=4,'fluid_1'=4,'fluid_2'=2,'solid'=4] {'solid'}, dimensions={0}, use_global_device_ids=true | all-gather | bytes 500 | tf_op jit(solution)/shard_map/all_gather | solution.py:16
  (386 shorter events, 346.1 us)
Async XLA Ops:
  25.9 16.8 %all-to-all-start.1 = ((bf16[128,2,768]{2,1,0:T(2,128)(2,1)}), bf16[128,2,768]{2,1,0:T(2,128)(2,1)S(1)}, u32[]{:S(2)}, u32[]{:S(2)}) async-start(bf16[128,2,768]{2,1,0:T(2,128)(2,1)} %reshape.224), calls=%async_computation.1 | async-start | bytes 786432 | tf_op jit(solution)/shard_map/all_to_all | solution.py:22
  52.1 24.4 %copy-start = (f32[8,768]{1,0:T(8,128)S(1)}, f32[8,768]{1,0:T(8,128)}, u32[]{:S(2)}) copy-start(f32[8,768]{1,0:T(8,128)} %param.14) | copy-start | bytes 73732
  52.2 24.4 %copy-start.1 = (f32[8,768]{1,0:T(8,128)S(1)}, f32[8,768]{1,0:T(8,128)}, u32[]{:S(2)}) copy-start(f32[8,768]{1,0:T(8,128)} %param.15) | copy-start | bytes 73732
  108.3 13.5 %copy-start.5 = (u32[128]{0:T(128)S(1)}, u32[128]{0:T(128)}, u32[]{:S(2)}) copy-start(u32[128]{0:T(128)} %constant.35) | copy-start | bytes 1540
  108.8 33.7 %copy-start.4 = (u32[128]{0:T(128)S(1)}, u32[128]{0:T(128)}, u32[]{:S(2)}) copy-start(u32[128]{0:T(128)} %constant.40) | copy-start | bytes 1540
  115.5 40.4 %copy-start.3 = (u32[128]{0:T(128)S(1)}, u32[128]{0:T(128)}, u32[]{:S(2)}) copy-start(u32[128]{0:T(128)} %constant.45) | copy-start | bytes 1540
  115.5 54.0 %copy-start.2 = (u32[128]{0:T(128)S(1)}, u32[128]{0:T(128)}, u32[]{:S(2)}) copy-start(u32[128]{0:T(128)} %constant.50) | copy-start | bytes 1540
  117.0 16.7 %all-to-all-start.4 = ((bf16[128,2,768]{2,1,0:T(2,128)(2,1)}), bf16[128,2,768]{2,1,0:T(2,128)(2,1)S(1)}, u32[]{:S(2)}, u32[]{:S(2)}) async-start(bf16[128,2,768]{2,1,0:T(2,128)(2,1)} %reshape.236), calls=%async_computation.4 | async-start | bytes 786432 | tf_op jit(solution)/shard_map/all_to_all | solution.py:22
  222.8 16.7 %all-to-all-start.6 = ((bf16[128,2,768]{2,1,0:T(2,128)(2,1)}), bf16[128,2,768]{2,1,0:T(2,128)(2,1)S(1)}, u32[]{:S(2)}, u32[]{:S(2)}) async-start(bf16[128,2,768]{2,1,0:T(2,128)(2,1)} %reshape.243), calls=%async_computation.6 | async-start | bytes 786432 | tf_op jit(solution)/shard_map/all_to_all | solution.py:22
  341.8 16.7 %all-to-all-start.8 = ((bf16[128,2,768]{2,1,0:T(2,128)(2,1)}), bf16[128,2,768]{2,1,0:T(2,128)(2,1)S(1)}, u32[]{:S(2)}, u32[]{:S(2)}) async-start(bf16[128,2,768]{2,1,0:T(2,128)(2,1)} %reshape.251), calls=%async_computation.8 | async-start | bytes 786432 | tf_op jit(solution)/shard_map/all_to_all | solution.py:22
  474.9 16.7 %all-to-all-start.10 = ((bf16[128,2,768]{2,1,0:T(2,128)(2,1)}), bf16[128,2,768]{2,1,0:T(2,128)(2,1)S(1)}, u32[]{:S(2)}, u32[]{:S(2)}) async-start(bf16[128,2,768]{2,1,0:T(2,128)(2,1)} %reshape.259), calls=%async_computation.10 | async-start | bytes 786432 | tf_op jit(solution)/shard_map/all_to_all | solution.py:22
  611.6 16.7 %all-to-all-start.12 = ((bf16[128,2,768]{2,1,0:T(2,128)(2,1)}), bf16[128,2,768]{2,1,0:T(2,128)(2,1)S(1)}, u32[]{:S(2)}, u32[]{:S(2)}) async-start(bf16[128,2,768]{2,1,0:T(2,128)(2,1)} %reshape.267), calls=%async_computation.12 | async-start | bytes 786432 | tf_op jit(solution)/shard_map/all_to_all | solution.py:22
